TPU v7x, 32 devices: a whole 2x2x4 slice. The times are simulated.
32 devices in a mesh: fsdp: 32 (over z, y, x, core).
Axes of the slice: x: 2, y: 2, z: 4, core: 2. Of those that a mesh axis runs over, the one named last changes fastest.
Arguments:
- images: bfloat16 [64, 197, 384], P('fsdp'), may hold values from -6 to 6
- cotangent: float32 [64, 197, 384], P('fsdp'), may hold values from -6 to 6
- counts: int32 [32], P('fsdp'), may hold values from 1 to 2, as said below
- params: float32 [2, 1777664], P(None, 'fsdp'), may hold values from -3 to 3, as said below
- moment_one: float32 [2, 1777664], P(None, 'fsdp'), may hold values from -12 to 12
- moment_two: float32 [2, 1777664], P(None, 'fsdp'), may hold values from 20 to 400
Outputs:
- outputs: float32 [64, 197, 384], P('fsdp')
- input_grad: float32 [64, 197, 384], P('fsdp')
- weight_grads: float32 [2, 1777664], P(None, 'fsdp')
- new_params: float32 [2, 1777664], P(None, 'fsdp')
- new_first: float32 [2, 1777664], P(None, 'fsdp')
- new_second: float32 [2, 1777664], P(None, 'fsdp')
Inputs may be any that keep to these rules, and one draw needn't show every extreme that they name: Each device's images fill its first counts slots, the others are empty; some device holds 2 images and some holds 1. `params`: each row is one layer's parameters in the order of the steps; entries past 1774080 are zero.
All inputs are finite; a program needn't handle non-finite values.
Results may differ from a plain program's by a relative error of at most 0.012.
The roundings to bfloat16 on the way count: a program that leaves them out, or rounds other values in their place, can miss the bound.
Values may be sent and summed in bfloat16 or wider, within the bound.
A program may use at most 128 MiB of HBM per device.

v0:
```python
import math

import jax
import jax.numpy as jnp
from jax import lax
from jax.sharding import PartitionSpec as P

D = 384
HEADS = 6
HEAD_DIM = 64
FF = 1536
SEQ = 197
LAYERS = 2
ADAM_STEP = 4


EPS_NORM = 1e-06
BETA_ONE = 0.9
BETA_TWO = 0.999
ADAM_EPS = 1e-08
DECAY = 0.05
LEARN = 0.2
INV_ROOT_TWO = 0.7071067811865476
INV_ROOT_TAU = 0.3989422804014327
LANES = 128


def layout():
    return [
        ("w_qkv", (D, 3 * D)),
        ("w_out", (D, D)),
        ("w_one", (D, FF)),
        ("w_two", (FF, D)),
        ("gain_one", (D,)),
        ("bias_one", (D,)),
        ("bias_query", (D,)),
        ("bias_value", (D,)),
        ("bias_out", (D,)),
        ("gain_two", (D,)),
        ("bias_two", (D,)),
        ("bias_hidden", (FF,)),
        ("bias_mlp", (D,)),
    ]


def unpack(flat_vec):
    pieces = {}
    offset = 0
    for param_name, param_shape in layout():
        entries = math.prod(param_shape)
        pieces[param_name] = flat_vec[offset : offset + entries].reshape(param_shape)
        offset = offset + entries
    return pieces


def pack(pieces, length_total):
    members = [pieces[param_name].reshape(-1) for param_name, param_shape in layout()]
    used = sum((member.shape[0] for member in members))
    members.append(jnp.zeros((length_total - used,), jnp.float32))
    return jnp.concatenate(members)


def project(left, right):
    return jnp.dot(left, right, preferred_element_type=jnp.float32)


def project_back(left, right):
    return lax.dot_general(
        left, right, (((1,), (1,)), ((), ())), preferred_element_type=jnp.float32
    )


def project_outer(left, right):
    return lax.dot_general(
        left, right, (((0,), (0,)), ((), ())), preferred_element_type=jnp.float32
    )


def batched(form, left, right):
    return jnp.einsum(form, left, right, preferred_element_type=jnp.float32)


def normalize(rows_in, gain_vec, shift_vec):
    centre = rows_in - jnp.mean(rows_in, axis=-1, keepdims=True)
    spread = lax.rsqrt(jnp.mean(centre * centre, axis=-1, keepdims=True) + EPS_NORM)
    normed = centre * spread
    return (normed, spread, normed * gain_vec.astype(jnp.float32) + shift_vec.astype(jnp.float32))


def normalize_back(upstream, normed, spread, gain_vec):
    scaled = upstream * gain_vec.astype(jnp.float32)
    centred = (
        scaled
        - jnp.mean(scaled, axis=-1, keepdims=True)
        - normed * jnp.mean(scaled * normed, axis=-1, keepdims=True)
    )
    return (spread * centred, jnp.sum(upstream * normed, axis=0), jnp.sum(upstream, axis=0))


def gelu_slope(pre_act):
    return 0.5 * (1.0 + lax.erf(pre_act * INV_ROOT_TWO)) + pre_act * INV_ROOT_TAU * jnp.exp(
        -0.5 * pre_act * pre_act
    )


def split_heads(rows_in):
    return rows_in.reshape(rows_in.shape[0] // SEQ, SEQ, HEADS, HEAD_DIM)


def attention_scores(query_rows, key_rows):
    return batched(
        "bqhc,bkhc->bhqk", split_heads(query_rows), split_heads(key_rows)
    ) * HEAD_DIM ** (-0.5)


def layer_forward(stream, weights):
    normed_one, spread_one, pre_one = normalize(stream, weights["gain_one"], weights["bias_one"])
    act_one = pre_one.astype(jnp.bfloat16)
    qkv_rows = project(act_one, weights["w_qkv"])
    query_rows = (qkv_rows[:, :D] + weights["bias_query"].astype(jnp.float32)).astype(jnp.bfloat16)
    key_rows = qkv_rows[:, D : 2 * D].astype(jnp.bfloat16)
    value_rows = (qkv_rows[:, 2 * D :] + weights["bias_value"].astype(jnp.float32)).astype(
        jnp.bfloat16
    )
    scores = attention_scores(query_rows, key_rows)
    row_max = jnp.max(scores, axis=-1, keepdims=True)
    log_total = row_max + jnp.log(jnp.sum(jnp.exp(scores - row_max), axis=-1, keepdims=True))
    attn_probs = jnp.exp(scores - log_total).astype(jnp.bfloat16)
    attended = (
        batched("bhqk,bkhc->bqhc", attn_probs, split_heads(value_rows))
        .reshape(-1, D)
        .astype(jnp.bfloat16)
    )
    middle = stream + project(attended, weights["w_out"]) + weights["bias_out"].astype(jnp.float32)
    normed_two, spread_two, pre_two = normalize(middle, weights["gain_two"], weights["bias_two"])
    act_two = pre_two.astype(jnp.bfloat16)
    hidden_pre = project(act_two, weights["w_one"]) + weights["bias_hidden"].astype(jnp.float32)
    hidden_act = jax.nn.gelu(hidden_pre, approximate=False).astype(jnp.bfloat16)
    result = (
        middle + project(hidden_act, weights["w_two"]) + weights["bias_mlp"].astype(jnp.float32)
    )
    saved = (
        normed_one,
        spread_one,
        act_one,
        query_rows,
        key_rows,
        value_rows,
        log_total,
        attended,
        normed_two,
        spread_two,
        act_two,
        hidden_pre,
        hidden_act,
    )
    return (result, saved)


def layer_backward(upstream, saved, weights):
    (
        normed_one,
        spread_one,
        act_one,
        query_rows,
        key_rows,
        value_rows,
        log_total,
        attended,
        normed_two,
        spread_two,
        act_two,
        hidden_pre,
        hidden_act,
    ) = saved
    grad_parts = {}
    up_bf = upstream.astype(jnp.bfloat16)
    grad_parts["w_two"] = project_outer(hidden_act, up_bf)
    grad_parts["bias_mlp"] = jnp.sum(upstream, axis=0)
    hidden_grad = project_back(up_bf, weights["w_two"]) * gelu_slope(hidden_pre)
    hidden_bf = hidden_grad.astype(jnp.bfloat16)
    grad_parts["w_one"] = project_outer(act_two, hidden_bf)
    grad_parts["bias_hidden"] = jnp.sum(hidden_grad, axis=0)
    norm_grad, grad_parts["gain_two"], grad_parts["bias_two"] = normalize_back(
        project_back(hidden_bf, weights["w_one"]), normed_two, spread_two, weights["gain_two"]
    )
    middle_grad = upstream + norm_grad
    middle_bf = middle_grad.astype(jnp.bfloat16)
    grad_parts["w_out"] = project_outer(attended, middle_bf)
    grad_parts["bias_out"] = jnp.sum(middle_grad, axis=0)
    attended_grad = project_back(middle_bf, weights["w_out"]).astype(jnp.bfloat16)
    heads_do = split_heads(attended_grad)
    attn_exact = jnp.exp(attention_scores(query_rows, key_rows) - log_total)
    attn_probs = attn_exact.astype(jnp.bfloat16)
    value_grad = batched("bhqk,bqhc->bkhc", attn_probs, heads_do).reshape(-1, D)
    prob_grad = batched("bqhc,bkhc->bhqk", heads_do, split_heads(value_rows))
    row_inner = jnp.sum(prob_grad * attn_exact, axis=-1, keepdims=True)
    score_grad = (attn_exact * (prob_grad - row_inner) * HEAD_DIM ** (-0.5)).astype(jnp.bfloat16)
    query_grad = batched("bhqk,bkhc->bqhc", score_grad, split_heads(key_rows)).reshape(-1, D)
    key_grad = batched("bhqk,bqhc->bkhc", score_grad, split_heads(query_rows)).reshape(-1, D)
    grad_parts["bias_query"] = jnp.sum(query_grad, axis=0)
    grad_parts["bias_value"] = jnp.sum(value_grad, axis=0)
    mixed_bf = jnp.concatenate([query_grad, key_grad, value_grad], axis=1).astype(jnp.bfloat16)
    grad_parts["w_qkv"] = project_outer(act_one, mixed_bf)
    in_grad, grad_parts["gain_one"], grad_parts["bias_one"] = normalize_back(
        project_back(mixed_bf, weights["w_qkv"]), normed_one, spread_one, weights["gain_one"]
    )
    return (middle_grad + in_grad, grad_parts)


def adamw(weights_in, first_in, second_in, grad_in):
    first_new = BETA_ONE * first_in + (1.0 - BETA_ONE) * grad_in
    second_new = BETA_TWO * second_in + (1.0 - BETA_TWO) * grad_in * grad_in
    first_hat = first_new / (1.0 - BETA_ONE**ADAM_STEP)
    second_hat = second_new / (1.0 - BETA_TWO**ADAM_STEP)
    updated = weights_in - LEARN * (
        first_hat / (jnp.sqrt(second_hat) + ADAM_EPS) + DECAY * weights_in
    )
    return (updated, first_new, second_new)


def as_tiles(shard_vec):
    return shard_vec.astype(jnp.bfloat16).reshape(-1, LANES)


def on_device(images, cotangent, counts, params, moment_one, moment_two):
    slot_count = images.shape[0]
    shard_len = params.shape[1]
    live = (jnp.arange(slot_count) < counts[0]).astype(jnp.float32)
    live_rows = jnp.repeat(live, SEQ)[:, None]
    flat_length = shard_len * lax.axis_size("fsdp")
    forward_w = []
    for position in range(LAYERS):
        gathered = lax.all_gather(as_tiles(params[position]), "fsdp", axis=0, tiled=True)
        forward_w.append(unpack(gathered.reshape(-1)))
    stream = images.reshape(-1, D).astype(jnp.float32)
    saves = []
    for position in range(LAYERS):
        stream, saved = layer_forward(stream, forward_w[position])
        saves.append(saved)
    output_rows = stream * live_rows
    backward_w = [
        unpack(lax.all_gather(as_tiles(params[position]), "fsdp", axis=0, tiled=True).reshape(-1))
        for position in range(LAYERS)
    ]
    upstream = cotangent.reshape(-1, D) * live_rows
    grad_shards = [None] * LAYERS
    for position in reversed(range(LAYERS)):
        upstream, grad_parts = layer_backward(upstream, saves[position], backward_w[position])
        flat_grad = pack(grad_parts, flat_length).reshape(-1, LANES)
        grad_shards[position] = lax.psum_scatter(
            flat_grad, "fsdp", scatter_dimension=0, tiled=True
        ).reshape(-1)
    grad_stack = jnp.stack(grad_shards)
    updated, first_new, second_new = adamw(params, moment_one, moment_two, grad_stack)
    return (
        output_rows.reshape(images.shape),
        upstream.reshape(images.shape),
        grad_stack,
        updated,
        first_new,
        second_new,
    )


def solution(mesh):
    placed = (
        P("fsdp", None, None),
        P("fsdp", None, None),
        P("fsdp"),
        P(None, "fsdp"),
        P(None, "fsdp"),
        P(None, "fsdp"),
    )
    return jax.shard_map(
        on_device,
        mesh=mesh,
        in_specs=placed,
        out_specs=(
            P("fsdp", None, None),
            P("fsdp", None, None),
            P(None, "fsdp"),
            P(None, "fsdp"),
            P(None, "fsdp"),
            P(None, "fsdp"),
        ),
        check_vma=False,
    )
```

profile of v0, /device:TPU:0, one launch (start us, length us, event | category | flops | bytes accessed | tf_op | source)
XLA Modules:
  0.0 570.9 jit_solution(9111548803270931515)
XLA Ops:
  18.1 56.3 %all-gather.5.cloned.1.call-done = bf16[32,434,128]{2,1,0:T(8,128)(2,1)} async-done(((bf16[1,434,128]{2,1,0:T(8,128)(2,1)}), bf16[32,434,128]{2,1,0:T(8,128)(2,1)}) %all-gather.5.cloned.1.call-update) | async-done | bytes 3555344 | tf_op jit(solution)/shard_map/all_gather | solution.py:234
  74.4 4.9 reshape.534
  81.4 3.2 fusion.154
  84.7 52.1 %all-gather.7.cloned.1.call-done = bf16[32,434,128]{2,1,0:T(8,128)(2,1)} async-done(((bf16[1,434,128]{2,1,0:T(8,128)(2,1)}), bf16[32,434,128]{2,1,0:T(8,128)(2,1)}) %all-gather.7.cloned.1.call-update) | async-done | bytes 3555344 | tf_op jit(solution)/shard_map/all_gather | solution.py:234
  136.7 4.7 reshape.536
  142.9 2.1 slice.200
  146.3 3.3 fusion.153
  162.3 3.5 reshape.484
  167.7 3.1 reshape.485
  170.8 2.9 reshape.486
  173.7 8.8 %fusion.6 = (bf16[394,1536]{1,0:T(8,128)(2,1)S(1)}, f32[394,1536]{1,0:T(8,128)}) fusion(f32[1536]{0:T(1024)S(1)} %fusion.113, bf16[384,1536]{1,0:T(8,128)(2,1)} %reshape.484, f32[394,384]{1,0:T(8,128)S(1)} %get-tuple-element.99, f32[384]{0:T(512)S(1)} %get-tuple-element.73, f32[384]{0:T(512)S(1)} %get-tuple-element.74, f32[394]{0:T(512)S(1)} %add_rsqrt_fusion.3, ...), kind=kOutput, calls=%fused_computation.12 | convolution fusion | flops 505479936 | bytes 5428304 | tf_op jit(solution)/shard_map/dot_general | solution.py:64
  182.5 2.4 fusion.160
  187.5 2.3 reshape.542
  189.8 2.2 copy.155
  194.9 2.5 reshape.544
  197.4 2.2 copy.154
  206.8 3.5 reshape.491
  212.9 3.1 reshape.492
  216.0 8.5 %fusion.9 = (bf16[394,1536]{1,0:T(8,128)(2,1)}, f32[394,1536]{1,0:T(8,128)S(1)}) fusion(f32[1536]{0:T(1024)S(1)} %copy-done.74, bf16[384,1536]{1,0:T(8,128)(2,1)} %reshape.491, f32[394,384]{1,0:T(8,128)} %copy-done.10, f32[384]{0:T(512)S(1)} %copy-done.71, f32[384]{0:T(512)S(1)} %get-tuple-element.64, f32[394]{0:T(512)S(1)} %add_rsqrt_fusion.1, ...), kind=kOutput, calls=%fused_computation.15 | convolution fusion | flops 505479936 | bytes 5428304 | tf_op jit(solution)/shard_map/dot_general | solution.py:64
  231.7 2.3 reshape.545
  234.1 2.2 copy.161
  236.3 3.0 fusion.169
  239.3 6.7 %fusion.158 = (f32[6,64]{1,0:T(8,128)}, bf16[2,197,6,64]{1,3,2,0:T(8,128)(2,1)}) fusion(bf16[2,197,6,64]{1,3,2,0:T(8,128)(2,1)} %copy.154, f32[2,6,197,197]{2,3,1,0:T(8,128)} %fusion.169, f32[2,6,197]{2,1,0:T(8,128)S(1)} %log_add_fusion, f32[2,6,197,197]{2,3,1,0:T(8,128)} %copy-done), kind=kOutput, calls=%fused_computation.286 | convolution fusion | flops 64106764 | bytes 4341840 | tf_op jit(solution)/shard_map/bhqk,bkhc->bqhc/dot_general | solution.py:80
  245.9 6.1 %fusion.71 = bf16[2,197,6,64]{1,3,2,0:T(8,128)(2,1)} fusion(bf16[2,197,6,64]{1,3,2,0:T(8,128)(2,1)} %copy-done.42, f32[2,6,197,197]{2,3,1,0:T(8,128)} %fusion.169, f32[2,6,197,197]{2,3,1,0:T(8,128)} %copy-done, f32[2,6,197]{2,1,0:T(8,128)S(1)} %log_add_fusion), kind=kOutput, calls=%fused_computation.93 | convolution fusion | flops 63955852 | bytes 4340304 | tf_op jit(solution)/shard_map/bhqk,bqhc->bkhc/dot_general | solution.py:80
  252.0 3.7 fusion.157
  269.6 3.3 multiply_reduce_fusion.5
  273.4 2.3 fusion.167
  279.4 2.5 reshape.546
  282.0 2.3 copy.173
  284.2 3.0 fusion.170
  287.2 5.1 fusion.156
  292.3 4.6 fusion.74
  301.6 2.4 fusion.87
  311.8 3.1 multiply_reduce_fusion.7
  318.3 2.3 fusion.83
  320.6 2.4 fusion.106
  323.1 2.6 fusion.92
  331.5 3.1 reshape.511
  334.7 3.3 reshape.512
  339.0 3.4 constant_dynamic-update-slice_fusion.29
  358.4 2.9 constant_dynamic-update-slice_fusion.6
  361.4 3.1 reshape.506
  364.5 3.2 reshape.507
  368.8 3.4 constant_dynamic-update-slice_fusion.28
  386.9 159.5 %fusion.148 = (f32[448,128]{1,0:T(8,128)S(1)}, f32[448,128]{1,0:T(8,128)S(1)}) fusion(f32[13888,128]{1,0:T(8,128)} %bitcast.190, f32[13888,128]{1,0:T(8,128)} %bitcast.191), kind=kCustom, calls=%all-reduce-scatter.2 | all-reduce-scatter fusion | flops 3670017 | bytes 14680064
  547.0 2.9 collective-permute-start.1
  550.6 4.3 collective-permute-start
  560.6 3.0 multiply_subtract_fusion
  (344 shorter events, 131.2 us)
Async XLA Ops:
  7.2 6.7 %copy-start.36 = (f32[2,197,384]{2,0,1:T(2,128)S(1)}, f32[2,197,384]{2,0,1:T(2,128)}, u32[]{:S(2)}) copy-start(f32[2,197,384]{2,0,1:T(2,128)} %param.7) | copy-start | bytes 1815556
  7.2 67.2 %all-gather.5.cloned.1.call-start = ((), (), s32[]{:S(2)}) async-start(), calls=%async_computation | async-start | bytes 3717120 | tf_op jit(solution)/shard_map/all_gather | solution.py:234
  10.3 126.4 %all-gather.7.cloned.1.call-start = ((), (), s32[]{:S(2)}) async-start(), calls=%async_computation.1 | async-start | bytes 3717120 | tf_op jit(solution)/shard_map/all_gather | solution.py:234
  13.0 3.8 copy-start.20
  81.4 92.2 %copy-start.69 = (f32[384]{0:T(512)}, f32[384]{0:T(512)S(1)}, u32[]{:S(2)}) copy-start(f32[384]{0:T(512)S(1)} %get-tuple-element.73) | copy-start | bytes 4612
  146.3 3.9 slice-start
  153.8 4.6 copy-start.24
  161.4 6.3 %copy-start.30 = (bf16[394,384]{0,1:T(8,128)(2,1)}, bf16[394,384]{0,1:T(8,128)(2,1)S(1)}, u32[]{:S(2)}) copy-start(bf16[394,384]{0,1:T(8,128)(2,1)S(1)} %convert_element_type.333) | copy-start | bytes 907780
  167.4 15.0 %copy-start.7 = (f32[394,384]{1,0:T(8,128)}, f32[394,384]{1,0:T(8,128)S(1)}, u32[]{:S(2)}) copy-start(f32[394,384]{1,0:T(8,128)S(1)} %get-tuple-element.99) | copy-start | bytes 1815556
  173.7 8.8 %copy-start.56 = (bf16[1536,384]{1,0:T(8,128)(2,1)S(1)}, bf16[1536,384]{1,0:T(8,128)(2,1)}, u32[]{:S(2)}) copy-start(bf16[1536,384]{1,0:T(8,128)(2,1)} %reshape.485) | copy-start | bytes 3538948
  173.7 8.8 %copy-start.82 = (f32[384]{0:T(512)S(1)}, f32[384]{0:T(512)}, u32[]{:S(2)}) copy-start(f32[384]{0:T(512)} %get-tuple-element.72) | copy-start | bytes 4612
  194.9 6.3 %copy-start.42 = (bf16[2,197,6,64]{1,3,2,0:T(8,128)(2,1)}, bf16[2,197,6,64]{1,3,2,0:T(8,128)(2,1)S(1)}, u32[]{:S(2)}) copy-start(bf16[2,197,6,64]{1,3,2,0:T(8,128)(2,1)S(1)} %copy.153) | copy-start | bytes 907780
  201.7 4.2 slice-start.2
  202.8 7.5 %copy-start.77 = (f32[384]{0:T(512)S(1)}, f32[384]{0:T(512)}, u32[]{:S(2)}) copy-start(f32[384]{0:T(512)} %get-tuple-element.65) | copy-start | bytes 4612
  206.8 3.5 copy-start.32
  211.8 4.2 copy-start.71
  211.8 4.2 copy-start.74
  212.9 13.7 %copy-start.66 = (f32[394]{0:T(512)}, f32[394]{0:T(512)S(1)}, u32[]{:S(2)}) copy-start(f32[394]{0:T(512)S(1)} %add_rsqrt_fusion.1) | copy-start | bytes 4732
  216.0 8.5 %copy-start.53 = (bf16[1536,384]{1,0:T(8,128)(2,1)S(1)}, bf16[1536,384]{1,0:T(8,128)(2,1)}, u32[]{:S(2)}) copy-start(bf16[1536,384]{1,0:T(8,128)(2,1)} %reshape.492) | copy-start | bytes 3538948
  216.0 8.5 %copy-start.65 = (bf16[394,384]{1,0:T(8,128)(2,1)S(1)}, bf16[394,384]{1,0:T(8,128)(2,1)}, u32[]{:S(2)}) copy-start(bf16[394,384]{1,0:T(8,128)(2,1)} %convert_element_type.376) | copy-start | bytes 907780
  226.6 4.0 copy-start.35
  228.1 8.2 %copy-start.27 = (bf16[2,197,6,64]{1,3,2,0:T(8,128)(2,1)S(1)}, bf16[2,197,6,64]{1,3,2,0:T(8,128)(2,1)}, u32[]{:S(2)}) copy-start(bf16[2,197,6,64]{1,3,2,0:T(8,128)(2,1)} %copy.155) | copy-start | bytes 907780
  245.9 6.1 %copy-start.28 = (bf16[2,197,6,64]{1,3,2,0:T(8,128)(2,1)S(1)}, bf16[2,197,6,64]{1,3,2,0:T(8,128)(2,1)}, u32[]{:S(2)}) copy-start(bf16[2,197,6,64]{1,3,2,0:T(8,128)(2,1)} %copy.161) | copy-start | bytes 907780
  252.0 3.7 copy-start.64
  255.7 9.0 %copy-start.44 = (bf16[2,197,6,64]{1,3,2,0:T(8,128)(2,1)S(1)}, bf16[2,197,6,64]{1,3,2,0:T(8,128)(2,1)}, u32[]{:S(2)}) copy-start(bf16[2,197,6,64]{1,3,2,0:T(8,128)(2,1)} %get-tuple-element.91) | copy-start | bytes 907780
  268.9 4.1 copy-start.5
  269.6 3.7 copy-start.57
  269.6 3.7 copy-start.89
  273.3 3.8 copy-start.18
  277.1 7.1 %copy-start.25 = (bf16[2,197,6,64]{1,3,2,0:T(8,128)(2,1)S(1)}, bf16[2,197,6,64]{1,3,2,0:T(8,128)(2,1)}, u32[]{:S(2)}) copy-start(bf16[2,197,6,64]{1,3,2,0:T(8,128)(2,1)} %copy-done.24) | copy-start | bytes 907780
  292.3 4.6 copy-start.29
  301.6 3.9 copy-start.62
  304.0 3.8 copy-start.43
  305.5 6.4 %copy-start.1 = (f32[394,384]{1,0:T(8,128)S(1)}, f32[394,384]{1,0:T(8,128)}, u32[]{:S(2)}) copy-start(f32[394,384]{1,0:T(8,128)} %reshape.514) | copy-start | bytes 1815556
  305.5 6.4 %copy-start.22 = (bf16[384,1152]{1,0:T(8,128)(2,1)S(1)}, bf16[384,1152]{1,0:T(8,128)(2,1)}, u32[]{:S(2)}) copy-start(bf16[384,1152]{1,0:T(8,128)(2,1)} %copy-done.21) | copy-start | bytes 2654212
  339.0 3.4 copy-start.13
  342.4 6.8 %copy-start.78 = (f32[384]{0:T(512)S(1)}, f32[384]{0:T(512)}, u32[]{:S(2)}) copy-start(f32[384]{0:T(512)} %get-tuple-element.60) | copy-start | bytes 4612
  342.4 8.1 %copy-start.84 = (f32[384]{0:T(512)S(1)}, f32[384]{0:T(512)}, u32[]{:S(2)}) copy-start(f32[384]{0:T(512)} %get-tuple-element.34) | copy-start | bytes 4612
  342.4 9.4 %copy-start.83 = (f32[384]{0:T(512)S(1)}, f32[384]{0:T(512)}, u32[]{:S(2)}) copy-start(f32[384]{0:T(512)} %get-tuple-element.44) | copy-start | bytes 4612
  342.4 10.7 %copy-start.75 = (f32[1536]{0:T(1024)S(1)}, f32[1536]{0:T(1024)}, u32[]{:S(2)}) copy-start(f32[1536]{0:T(1024)} %get-tuple-element.118) | copy-start | bytes 18436
  342.4 12.0 %copy-start.73 = (f32[384]{0:T(512)S(1)}, f32[384]{0:T(512)}, u32[]{:S(2)}) copy-start(f32[384]{0:T(512)} %get-tuple-element.94) | copy-start | bytes 4612
  342.4 14.6 %copy-start.15 = (f32[384,1152]{1,0:T(8,128)S(1)}, f32[384,1152]{1,0:T(8,128)}, u32[]{:S(2)}) copy-start(f32[384,1152]{1,0:T(8,128)} %fusion.93) | copy-start | bytes 5308420
  372.2 8.1 %copy-start.86 = (f32[384]{0:T(512)S(1)}, f32[384]{0:T(512)}, u32[]{:S(2)}) copy-start(f32[384]{0:T(512)} %get-tuple-element.30) | copy-start | bytes 4612
  372.2 9.4 %copy-start.85 = (f32[384]{0:T(512)S(1)}, f32[384]{0:T(512)}, u32[]{:S(2)}) copy-start(f32[384]{0:T(512)} %get-tuple-element.42) | copy-start | bytes 4612
  372.2 10.7 %copy-start.76 = (f32[1536]{0:T(1024)S(1)}, f32[1536]{0:T(1024)}, u32[]{:S(2)}) copy-start(f32[1536]{0:T(1024)} %get-tuple-element.120) | copy-start | bytes 18436
  386.9 168.1 %copy-start.59 = (f32[394,384]{1,0:T(8,128)S(1)}, f32[394,384]{1,0:T(8,128)}, u32[]{:S(2)}) copy-start(f32[394,384]{1,0:T(8,128)} %get-tuple-element.117) | copy-start | bytes 1815556
  547.0 11.7 %collective-permute-start.1 = (f32[434,128]{1,0:T(8,128)}, f32[434,128]{1,0:T(8,128)S(1)}, u32[]{:S(2)}, u32[]{:S(2)}) collective-permute-start(f32[434,128]{1,0:T(8,128)} %slice.215), channel_id=1, source_target_pairs={{0,1},{1,2},{2,3},{3,4},{4,5},{5,6},{6,7},{7,8},{8,9},{9,10},{10,1... | collective-permute-start | bytes 666632
  550.6 9.0 %collective-permute-start = (f32[434,128]{1,0:T(8,128)}, f32[434,128]{1,0:T(8,128)S(1)}, u32[]{:S(2)}, u32[]{:S(2)}) collective-permute-start(f32[434,128]{1,0:T(8,128)} %slice.214), channel_id=1, source_target_pairs={{0,1},{1,2},{2,3},{3,4},{4,5},{5,6},{6,7},{7,8},{8,9},{9,10},{10,1... | collective-permute-start | bytes 666632
  (49 other events, 122.3 us)
Sparse Core Ops, SparseCore 0:
  11.5 62.8 all-gather.4
  77.9 58.8 all-gather.6
where the time goes:
time: 577 us; the launch traced here: 571 us
  local copies, waits for them, and re-layouts  166 us (29%)
  blocking collectives  159 us (28%)
  waiting for transfers between devices  109 us (19%)
  matrix products  96.3 us (17%)
  other arithmetic  16.9 us (3%)
  between operations  16.2 us (3%)
  starting transfers between devices  7.25 us (1%)
    unnamed x1, blocking collectives  159 us
    all_gather x2, waiting for transfers between devices, on_device(): lax.all_gather(as_tiles(params[position]), 'fsdp', axis=0, tiled=True)  108 us
    unnamed x225, local copies, waits for them, and re-layouts  63 us
    dot_general x12, matrix products, batched(): return jnp.einsum(form, left, right, preferred_element_type=jnp.float32)  37.7 us
    dot_general x8, matrix products, project(): return jnp.dot(left, right, preferred_element_type=jnp.float32)  26.3 us
    reshape x16, local copies, waits for them, and re-layouts, split_heads(): return rows_in.reshape(rows_in.shape[0] // SEQ, SEQ, HEADS, HEAD_DIM)  24.8 us
    reshape x8, local copies, waits for them, and re-layouts, unpack(): pieces[param_name] = flat_vec[offset:offset + entries].reshape(param_shape)  18.7 us
    reshape x8, local copies, waits for them, and re-layouts, pack(): pieces[param_name].reshape(-1)  16.7 us
  transfers between devices with their start and end apart: 4, of which 2 were waited for; matrix products, arithmetic and copies ran while one was open for 4% of the time, Pallas kernels for 0%

commit v1 on v0

v1 whole, which is shorter than its diff:
```python
import functools
import math

import jax
import jax.numpy as jnp
from jax import lax
from jax.experimental import pallas as pl
from jax.experimental.pallas import tpu as pltpu
from jax.sharding import PartitionSpec as P

D = 384
HEADS = 6
HEAD_DIM = 64
FF = 1536
SEQ = 197
LAYERS = 2
ADAM_STEP = 4

EPS_NORM = 1e-06
BETA_ONE = 0.9
BETA_TWO = 0.999
ADAM_EPS = 1e-08
DECAY = 0.05
LEARN = 0.2
INV_ROOT_TWO = 0.7071067811865476
INV_ROOT_TAU = 0.3989422804014327
LANES = 128
ROWS = 208
SUB = D // LANES
CHUNKS = FF // D
F32 = jnp.float32
BF16 = jnp.bfloat16

AT_OUT = 3 * D * SUB
AT_ONE = AT_OUT + D * SUB
AT_TWO = AT_ONE + D * SUB * CHUNKS
AT_SMALL = AT_TWO + D * SUB * CHUNKS
BLOCKS = 4 + 2 * CHUNKS
G_ONE, B_ONE, B_QUERY, B_VALUE, B_OUT, G_TWO, B_TWO, B_HIDDEN = range(8)
B_MLP = B_HIDDEN + CHUNKS
VECTORS = B_MLP + 1
USED = AT_SMALL + VECTORS * SUB


def nn(left, right):
    return jnp.dot(left, right, preferred_element_type=F32)


def nt(left, right):
    return lax.dot_general(left, right, (((1,), (1,)), ((), ())), preferred_element_type=F32)


def tn(left, right):
    return lax.dot_general(left, right, (((0,), (0,)), ((), ())), preferred_element_type=F32)


def block_rows(block, tile):
    if block < 3:
        return block * SUB + tile, 3 * SUB
    if block == 3:
        return AT_OUT + tile, SUB
    if block < 4 + CHUNKS:
        return AT_ONE + (block - 4) * SUB + tile, CHUNKS * SUB
    return AT_TWO + (block - 4 - CHUNKS) * D * SUB + tile, SUB


def unpack(gathered, flat, mats, vecs):
    devices, rows = gathered.shape[0], gathered.shape[1]

    def widen(device, carry):
        flat[pl.ds(device * rows, rows), :] = gathered[device].astype(F32)
        return carry

    lax.fori_loop(0, devices, widen, 0)
    for block in range(BLOCKS):
        for tile in range(SUB):
            start, stride = block_rows(block, tile)
            mats[block, :, tile * LANES : (tile + 1) * LANES] = flat[
                pl.ds(start, D, stride=stride), :
            ].astype(BF16)
    for vector in range(VECTORS):
        for tile in range(SUB):
            row = AT_SMALL + vector * SUB + tile
            vecs[vector : vector + 1, tile * LANES : (tile + 1) * LANES] = flat[row : row + 1, :]


def put_block(flat, block, value):
    for tile in range(SUB):
        start, stride = block_rows(block, tile)
        flat[pl.ds(start, D, stride=stride), :] = value[:, tile * LANES : (tile + 1) * LANES]


def put_vector(flat, vector, value):
    for tile in range(SUB):
        row = AT_SMALL + vector * SUB + tile
        flat[row : row + 1, :] = value[:, tile * LANES : (tile + 1) * LANES]


def col_sum(value):
    return jnp.sum(value, axis=0, keepdims=True)


def normalize(rows_in):
    centre = rows_in - jnp.mean(rows_in, axis=-1, keepdims=True)
    spread = lax.rsqrt(jnp.mean(centre * centre, axis=-1, keepdims=True) + EPS_NORM)
    return centre * spread, spread


def normalize_back(upstream, normed, spread, gain_vec):
    scaled = upstream * gain_vec
    centred = (
        scaled
        - jnp.mean(scaled, axis=-1, keepdims=True)
        - normed * jnp.mean(scaled * normed, axis=-1, keepdims=True)
    )
    return spread * centred


def lane_pick(half):
    lane = lax.broadcasted_iota(jnp.int32, (ROWS, LANES), 1)
    return (lane < HEAD_DIM) if half == 0 else (lane >= HEAD_DIM)


def pick(value, half):
    return jnp.where(lane_pick(half), value, jnp.zeros_like(value))


def forward(slots, stream, mats, vecs, saves):
    query, key, value, attended, exact, middle, slope, hidden = saves

    def vec(index):
        return vecs[index : index + 1, :]

    normed, _ = normalize(stream[...].astype(F32))
    act = (normed * vec(G_ONE) + vec(B_ONE)).astype(BF16)
    query[...] = (nn(act, mats[0]) + vec(B_QUERY)).astype(BF16)
    key[...] = nn(act, mats[1]).astype(BF16)
    value[...] = (nn(act, mats[2]) + vec(B_VALUE)).astype(BF16)

    def heads(pair, carry):
        lanes = pl.ds(pl.multiple_of(pair * LANES, LANES), LANES)
        inside = lax.broadcasted_iota(jnp.int32, (ROWS, ROWS), 1) < SEQ
        for slot in range(slots):
            rows = pl.ds(slot * ROWS, ROWS)
            q_pair, k_pair, v_pair = query[rows, lanes], key[rows, lanes], value[rows, lanes]
            total = jnp.zeros((ROWS, LANES), F32)
            for half in range(2):
                scores = nt(pick(q_pair, half), k_pair) * HEAD_DIM ** (-0.5)
                scores = jnp.where(inside, scores, -1e30)
                expd = jnp.exp(scores - jnp.max(scores, axis=-1, keepdims=True))
                probs = expd * (1.0 / jnp.sum(expd, axis=-1, keepdims=True))
                exact[pair * (2 * slots) + 2 * slot + half] = probs
                total += pick(nn(probs.astype(BF16), v_pair), half)
            attended[rows, lanes] = total.astype(BF16)
        return carry

    lax.fori_loop(0, HEADS // 2, heads, 0)
    middle[...] = stream[...].astype(F32) + nn(attended[...], mats[3]) + vec(B_OUT)
    normed, _ = normalize(middle[...])
    act = (normed * vec(G_TWO) + vec(B_TWO)).astype(BF16)

    result = middle[...] + vec(B_MLP)
    for chunk in range(CHUNKS):
        pre = nn(act, mats[4 + chunk]) + vec(B_HIDDEN + chunk)
        below = 0.5 * (1.0 + lax.erf(pre * INV_ROOT_TWO))
        hidden[chunk] = (pre * below).astype(BF16)
        slope[chunk] = below + pre * INV_ROOT_TAU * jnp.exp(-0.5 * pre * pre)
        result += nn(hidden[chunk], mats[4 + CHUNKS + chunk])
    return result


def backward(slots, upstream, stream, mats, vecs, saves, flat, mixed, att_grad):
    query, key, value, attended, exact, middle, slope, hidden = saves

    def vec(index):
        return vecs[index : index + 1, :]

    grad = upstream[...]
    up_bf = grad.astype(BF16)
    put_vector(flat, B_MLP, col_sum(grad))
    normed, spread = normalize(middle[...])
    act = (normed * vec(G_TWO) + vec(B_TWO)).astype(BF16)
    into = jnp.zeros_like(grad)
    for chunk in range(CHUNKS):
        hidden_grad = nt(up_bf, mats[4 + CHUNKS + chunk]) * slope[chunk]
        hidden_bf = hidden_grad.astype(BF16)
        put_vector(flat, B_HIDDEN + chunk, col_sum(hidden_grad))
        put_block(flat, 4 + CHUNKS + chunk, tn(hidden[chunk], up_bf))
        put_block(flat, 4 + chunk, tn(act, hidden_bf))
        into += nt(hidden_bf, mats[4 + chunk])
    put_vector(flat, G_TWO, col_sum(into * normed))
    put_vector(flat, B_TWO, col_sum(into))
    middle[...] = grad + normalize_back(into, normed, spread, vec(G_TWO))
    middle_bf = middle[...].astype(BF16)
    put_vector(flat, B_OUT, col_sum(middle[...]))
    put_block(flat, 3, tn(attended[...], middle_bf))
    att_grad[...] = nt(middle_bf, mats[3]).astype(BF16)

    def heads(pair, carry):
        lanes = pl.ds(pl.multiple_of(pair * LANES, LANES), LANES)
        q_sum = jnp.zeros((1, LANES), F32)
        v_sum = jnp.zeros((1, LANES), F32)
        for slot in range(slots):
            rows = pl.ds(slot * ROWS, ROWS)
            q_pair, k_pair, v_pair = query[rows, lanes], key[rows, lanes], value[rows, lanes]
            out_pair = att_grad[rows, lanes]
            q_grad = jnp.zeros((ROWS, LANES), F32)
            k_grad = jnp.zeros((ROWS, LANES), F32)
            v_grad = jnp.zeros((ROWS, LANES), F32)
            for half in range(2):
                probs = exact[pair * (2 * slots) + 2 * slot + half]
                out_half = pick(out_pair, half)
                v_grad += tn(probs.astype(BF16), out_half)
                prob_grad = nt(out_half, v_pair)
                inner = jnp.sum(prob_grad * probs, axis=-1, keepdims=True)
                score_grad = (probs * (prob_grad - inner) * HEAD_DIM ** (-0.5)).astype(BF16)
                q_grad += nn(score_grad, pick(k_pair, half))
                k_grad += tn(score_grad, pick(q_pair, half))
            q_sum += col_sum(q_grad)
            v_sum += col_sum(v_grad)
            mixed[0, rows, lanes] = q_grad.astype(BF16)
            mixed[1, rows, lanes] = k_grad.astype(BF16)
            mixed[2, rows, lanes] = v_grad.astype(BF16)
        flat[pl.ds(AT_SMALL + B_QUERY * SUB + pair, 1), :] = q_sum
        flat[pl.ds(AT_SMALL + B_VALUE * SUB + pair, 1), :] = v_sum
        return carry

    lax.fori_loop(0, HEADS // 2, heads, 0)
    normed, spread = normalize(stream[...].astype(F32))
    act = (normed * vec(G_ONE) + vec(B_ONE)).astype(BF16)
    into = jnp.zeros_like(grad)
    for part in range(3):
        put_block(flat, part, tn(act, mixed[part]))
        into += nt(mixed[part], mats[part])
    put_vector(flat, G_ONE, col_sum(into * normed))
    put_vector(flat, B_ONE, col_sum(into))
    return middle[...] + normalize_back(into, normed, spread, vec(G_ONE))


def send_out(flat, packed):
    devices, rows = packed.shape[0], packed.shape[1]
    owned = flat.shape[0] // devices
    flat[USED:, :] = jnp.zeros((flat.shape[0] - USED, LANES), F32)

    def narrow(device, carry):
        packed[device, :owned, :] = flat[pl.ds(device * owned, owned), :].astype(BF16)
        if rows > owned:
            packed[device, owned:, :] = jnp.zeros((rows - owned, LANES), BF16)
        return carry

    lax.fori_loop(0, devices, narrow, 0)


def save_shapes(slots):
    tokens = slots * ROWS
    return [
        ((tokens, D), BF16),
        ((tokens, D), BF16),
        ((tokens, D), BF16),
        ((tokens, D), BF16),
        ((HEADS * slots, ROWS, ROWS), F32),
        ((tokens, D), F32),
        ((CHUNKS, tokens, D), F32),
        ((CHUNKS, tokens, D), BF16),
    ]


WEIGHTS = [((BLOCKS, D, D), BF16), ((16, D), F32)]


def first_kernel(slots, gathered, stream, *rest):
    mats, vecs, *saves = rest[:10]
    result, flat = rest[10:]
    unpack(gathered, flat, mats, vecs)
    result[...] = forward(slots, stream, mats, vecs, saves)


def turn_kernel(slots, gathered, stream, upstream, result, down, packed, *rest):
    flat, mixed, att_grad, mats, vecs, *saves = rest
    unpack(gathered, flat, mats, vecs)
    result[...] = forward(slots, stream, mats, vecs, saves)
    down[...] = backward(
        slots, upstream, stream, mats, vecs, saves, flat, mixed, att_grad
    )
    send_out(flat, packed)


def last_kernel(slots, upstream, stream, *rest):
    mats, vecs, *saved = rest[:10]
    down, packed, flat, mixed, att_grad, middle = rest[10:]
    middle[...] = saved[5][...]
    saved[5] = middle
    down[...] = backward(
        slots, upstream, stream, mats, vecs, saved, flat, mixed, att_grad
    )
    send_out(flat, packed)


def shapes(listed):
    return [jax.ShapeDtypeStruct(extent, kind) for extent, kind in listed]


def scratch(listed):
    return [pltpu.VMEM(extent, kind) for extent, kind in listed]


def call(body, args, outs, scratches, flops):
    whole = pl.BlockSpec(memory_space=pltpu.VMEM)
    return pl.pallas_call(
        body,
        out_shape=shapes(outs),
        in_specs=[whole] * len(args),
        out_specs=[whole] * len(outs),
        scratch_shapes=scratch(scratches),
        cost_estimate=pl.CostEstimate(flops=flops, bytes_accessed=12000000, transcendentals=0),
        compiler_params=pltpu.CompilerParams(vmem_limit_bytes=60000000),
    )(*args)


def adamw(weights_in, first_in, second_in, grad_in):
    first_new = BETA_ONE * first_in + (1.0 - BETA_ONE) * grad_in
    second_new = BETA_TWO * second_in + (1.0 - BETA_TWO) * grad_in * grad_in
    first_hat = first_new / (1.0 - BETA_ONE**ADAM_STEP)
    second_hat = second_new / (1.0 - BETA_TWO**ADAM_STEP)
    updated = weights_in - LEARN * (
        first_hat / (jnp.sqrt(second_hat) + ADAM_EPS) + DECAY * weights_in
    )
    return (updated, first_new, second_new)


def as_tiles(shard_vec):
    return shard_vec.astype(jnp.bfloat16).reshape(-1, LANES)


def on_device(images, cotangent, counts, params, moment_one, moment_two):
    slots = images.shape[0]
    shard_len = params.shape[1]
    devices = lax.axis_size("fsdp")
    owned = shard_len // LANES
    padded = -(-owned // 16) * 16
    tokens = slots * ROWS
    flat_rows = owned * devices
    live = (jnp.arange(slots) < counts[0]).astype(F32)[:, None, None]
    gathered = [
        lax.all_gather(as_tiles(params[position]), "fsdp", axis=0) for position in range(LAYERS)
    ]
    widen = ((0, 0), (0, ROWS - SEQ), (0, 0))
    start = jnp.pad(images, widen).reshape(tokens, D)
    upstream = jnp.pad(cotangent * live, widen).reshape(tokens, D)

    saves = save_shapes(slots)
    rows_out = ((tokens, D), F32)
    packed_out = ((devices, padded, LANES), BF16)
    flat = ((flat_rows, LANES), F32)
    back = [flat, ((3, tokens, D), BF16), ((tokens, D), BF16)]
    flops = 2 * tokens * USED * LANES

    *kept, stream = call(
        functools.partial(first_kernel, slots),
        [gathered[0], start],
        WEIGHTS + saves + [rows_out],
        [flat],
        flops,
    )
    result, down, packed_one = call(
        functools.partial(turn_kernel, slots),
        [gathered[1], stream, upstream],
        [rows_out, rows_out, packed_out],
        back + WEIGHTS + saves,
        3 * flops,
    )
    down, packed_zero = call(
        functools.partial(last_kernel, slots),
        [down, start] + kept,
        [rows_out, packed_out],
        back + [rows_out],
        2 * flops,
    )
    grad_stack = jnp.stack(
        [
            lax.psum_scatter(
                packed.reshape(devices * padded, LANES), "fsdp", scatter_dimension=0, tiled=True
            )[:owned]
            .astype(F32)
            .reshape(-1)
            for packed in (packed_zero, packed_one)
        ]
    )
    updated, first_new, second_new = adamw(params, moment_one, moment_two, grad_stack)
    return (
        result.reshape(slots, ROWS, D)[:, :SEQ] * live,
        down.reshape(slots, ROWS, D)[:, :SEQ],
        grad_stack,
        updated,
        first_new,
        second_new,
    )


def solution(mesh):
    placed = (
        P("fsdp", None, None),
        P("fsdp", None, None),
        P("fsdp"),
        P(None, "fsdp"),
        P(None, "fsdp"),
        P(None, "fsdp"),
    )
    return jax.shard_map(
        on_device,
        mesh=mesh,
        in_specs=placed,
        out_specs=(
            P("fsdp", None, None),
            P("fsdp", None, None),
            P(None, "fsdp"),
            P(None, "fsdp"),
            P(None, "fsdp"),
            P(None, "fsdp"),
        ),
        check_vma=False,
    )
```

time: 577 us -> 449 us (0.78); the launches traced: 571 us -> 449 us
  waiting for transfers between devices: 109 us -> 367 us
  blocking collectives: 159 us -> 0 us
  local copies, waits for them, and re-layouts: 166 us -> 9.06 us
  matrix products: 96.3 us -> 0 us
  Pallas kernels: 0 us -> 51.1 us
  other arithmetic: 16.9 us -> 6.69 us
  starting transfers between devices: 7.25 us -> 0.38 us
    reduce_scatter x0 -> x2, waiting for transfers between devices: none -> 258 us  [on_device(): lax.psum_scatter(packed.reshape(devices * padded, LANES), 'fsdp', scatter...]
    unnamed x1 -> x0, blocking collectives: 159 us -> none
    dot_general x36 -> x0, matrix products: 96.3 us -> none  [the longest x12 37.7 us: batched(): return jnp.einsum(form, left, right, preferred_element_type=jnp.float32)]
    reshape x41 -> x0, local copies, waits for them, and re-layouts: 70.3 us -> none  [the longest x16 24.8 us: split_heads(): return rows_in.reshape(rows_in.shape[0] // SEQ, SEQ, HEADS, HEAD_DIM)]
    unnamed x225 -> x17, local copies, waits for them, and re-layouts: 63 us -> 5.52 us
    pallas_call x0 -> x3, Pallas kernels: none -> 51.1 us  [call(): pl.pallas_call(body, out_shape=shapes(outs), in_specs=[whole] * len(args)...]
    slice x11 -> x2, local copies, waits for them, and re-layouts: 10.2 us -> 0.08 us  [the longest x1 0.04 us: on_device(): result.reshape(slots, ROWS, D)[:, :SEQ] * live]
    convert_element_type x10 -> x0, local copies, waits for them, and re-layouts: 8.34 us -> none  [the longest x4 5.52 us: layer_forward(): attended = batched('bhqk,bkhc->bqhc', attn_probs, split_heads(value_rows)...]
  transfers between devices with their start and end apart: 4 -> 4, of which waited for: 2 -> 4; matrix products, arithmetic and copies ran while one was open for 4% -> 2% of each run, Pallas kernels for 0% -> 6%
where the time goes in v1:
time: 449 us
  waiting for transfers between devices  367 us (82%)
  Pallas kernels  51.1 us (11%)
  between operations  14.5 us (3%)
  local copies, waits for them, and re-layouts  9.06 us (2%)
  other arithmetic  6.69 us (1%)
    reduce_scatter x2, waiting for transfers between devices, on_device(): lax.psum_scatter(packed.reshape(devices * padded, LANES), 'fsdp', scatter...  258 us
    all_gather x2, waiting for transfers between devices, on_device(): lax.all_gather(as_tiles(params[position]), 'fsdp', axis=0)  109 us
    pallas_call x3, Pallas kernels, call(): pl.pallas_call(body, out_shape=shapes(outs), in_specs=[whole] * len(args)...  51.1 us
  transfers between devices with their start and end apart: 4, of which 4 were waited for; matrix products, arithmetic and copies ran while one was open for 2% of the time, Pallas kernels for 6%

profile of v1, /device:TPU:0, one launch (start us, length us, event | category | flops | bytes accessed | tf_op | source)
XLA Modules:
  0.0 449.1 jit_solution(1419946608955025124)
XLA Ops:
  7.2 0.0 all-gather.5.cloned.1.call-start
  7.2 1.2 convert.7
  8.4 1.8 slice_reduce_fusion
  10.2 0.0 all-gather.5.cloned.1.call-update
  10.2 0.0 all-gather.3.cloned.1.call-start
  10.3 0.7 all-gather.3.cloned.1.call-update
  11.0 0.0 reduce-scatter.5.cloned.1.call-start
  11.7 1.0 copy.22
  12.7 1.3 broadcast_multiply_fusion
  14.1 0.8 pad.8.clone
  14.9 0.9 pad.9.clone
  15.7 58.6 %all-gather.5.cloned.1.call-done.gathered = bf16[32,434,128]{2,1,0:T(8,128)(2,1)} async-done(((bf16[1,434,128]{2,1,0:T(8,128)(2,1)}), bf16[32,434,128]{2,1,0:T(8,128)(2,1)}) %all-gather.5.cloned.1.call-update) | async-done | bytes 3555344 | tf_op jit(solution)/shard_map/all_gather | solution.py:345
  74.3 12.4 %shard_map.109 = (bf16[12,384,384]{2,1,0:T(8,128)(2,1)}, f32[16,384]{1,0:T(8,128)}, bf16[416,384]{1,0:T(8,128)(2,1)}, bf16[416,384]{1,0:T(8,128)(2,1)}, bf16[416...) custom-call(bf16[32,434,128]{2,1,0:T(8,128)(2,1)} %all-gather.5.clon, ...), custom_call_target="tpu_custom_call" | custom-call | flops 1476034560 | bytes 12000000 | tf_op jit(solution)/shard_map/pallas_call | solution.py:309
  86.7 49.9 %all-gather.3.cloned.1.call-done.gathered = bf16[32,434,128]{2,1,0:T(8,128)(2,1)} async-done(((bf16[1,434,128]{2,1,0:T(8,128)(2,1)}), bf16[32,434,128]{2,1,0:T(8,128)(2,1)}) %all-gather.3.cloned.1.call-update) | async-done | bytes 3555344 | tf_op jit(solution)/shard_map/all_gather | solution.py:345
  136.7 22.4 %shard_map.110 = (f32[416,384]{1,0:T(8,128)}, f32[416,384]{1,0:T(8,128)}, bf16[32,448,128]{2,1,0:T(8,128)(2,1)}) custom-call(bf16[32,434,128]{2,1,0:T(8,128)(2,1)} %all-gather.3.cloned.1.call-done.gathered, f32[416,384]{1,0:T(8,128)} %get-tuple-element.22.stream, f32[416,384]{1,0:T(8,128)} %bitcast.28), custom_call_target="tpu_custom_call" | custom-call | flops 4428103680 | bytes 12000000 | tf_op jit(solution)/shard_map/pallas_call | solution.py:309
  159.0 0.0 reduce-scatter.5.cloned.1.call-update
  159.0 0.3 reduce-scatter.3.cloned.1.call-start
  159.3 16.4 %shard_map.111 = (f32[416,384]{1,0:T(8,128)}, bf16[32,448,128]{2,1,0:T(8,128)(2,1)}) custom-call(f32[416,384]{1,0:T(8,128)} %get-tuple-element.24.upstream, bf16[416,384]{1,0:T(8,128)(2,1)} %bitcast.25, bf16[12,384,384]{2,1,0:T(8,128)(2,1)} %get-tuple-element.25.rest_0_, f32[16,384]{1,0:T(8,128)} %get-tuple-element.26.rest_1_, ...), custom_call_target="tpu_custom_call" | custom-call | flops 2952069120 | bytes 12000000 | tf_op jit(solution)/shard_map/pallas_call | solution.py:309
  175.7 0.0 copy-start.1
  175.7 0.0 copy-start.2
  175.7 0.0 reduce-scatter.3.cloned.1.call-update
  175.7 0.0 copy-start
  175.7 0.0 copy-start.3
  175.7 0.0 copy-start.4
  175.7 1.0 copy-done.1
  176.8 0.1 copy-done.2
  177.0 1.1 copy.21
  178.1 1.2 copy_multiply_fusion
  179.3 119.9 %reduce-scatter.5.cloned.1.call-done = bf16[448,128]{1,0:T(8,128)(2,1)} async-done(((bf16[14336,128]{1,0:T(8,128)(2,1)}), bf16[448,128]{1,0:T(8,128)(2,1)}) %reduce-scatter.5.cloned.1.call-update) | async-done | bytes 114704 | tf_op jit(solution)/shard_map/reduce_scatter | solution.py:381
  299.2 0.9 slice_bitcast_fusion
  300.1 0.2 copy.29
  300.3 138.2 %reduce-scatter.3.cloned.1.call-done = bf16[448,128]{1,0:T(8,128)(2,1)} async-done(((bf16[14336,128]{1,0:T(8,128)(2,1)}), bf16[448,128]{1,0:T(8,128)(2,1)}) %reduce-scatter.3.cloned.1.call-update) | async-done | bytes 114704 | tf_op jit(solution)/shard_map/reduce_scatter | solution.py:381
  438.5 0.9 slice_bitcast_fusion.1
  439.4 0.2 copy.30
  439.5 0.0 copy-done
  439.5 0.0 copy-done.3
  439.6 0.0 copy-done.4
  439.6 3.0 multiply_subtract_fusion
  (4 shorter events, 0.1 us)
Async XLA Ops:
  7.2 67.2 %all-gather.5.cloned.1.call-start = ((), (), s32[]{:S(2)}) async-start(), calls=%async_computation.3 | async-start | bytes 3717120 | tf_op jit(solution)/shard_map/all_gather | solution.py:345
  10.2 126.4 %all-gather.3.cloned.1.call-start = ((), (), s32[]{:S(2)}) async-start(), calls=%async_computation.2 | async-start | bytes 3717120 | tf_op jit(solution)/shard_map/all_gather | solution.py:345
  11.0 288.2 %reduce-scatter.5.cloned.1.call-start = ((), (), s32[]{:S(2)}) async-start(), calls=%async_computation.5 | async-start | bytes 3784704 | tf_op jit(solution)/shard_map/reduce_scatter | solution.py:381
  159.0 279.4 %reduce-scatter.3.cloned.1.call-start = ((), (), s32[]{:S(2)}) async-start(), calls=%async_computation.4 | async-start | bytes 3784704 | tf_op jit(solution)/shard_map/reduce_scatter | solution.py:381
  175.7 1.1 copy-start.1
  175.7 1.3 copy-start.2
  175.7 263.8 %copy-start = (f32[2,55552]{1,0:T(2,128)S(1)}, f32[2,55552]{1,0:T(2,128)}, u32[]{:S(2)}) copy-start(f32[2,55552]{1,0:T(2,128)} %param.9) | copy-start | bytes 1333252
  175.7 263.8 %copy-start.3 = (f32[2,55552]{1,0:T(2,128)S(1)}, f32[2,55552]{1,0:T(2,128)}, u32[]{:S(2)}) copy-start(f32[2,55552]{1,0:T(2,128)} %param.10) | copy-start | bytes 1333252
  175.7 263.8 %copy-start.4 = (f32[2,55552]{1,0:T(2,128)S(1)}, f32[2,55552]{1,0:T(2,128)}, u32[]{:S(2)}) copy-start(f32[2,55552]{1,0:T(2,128)} %param.11) | copy-start | bytes 1333252
Sparse Core Ops, SparseCore 0:
  11.4 62.8 all-gather.4
  77.8 58.8 all-gather.2
  159.2 139.9 reduce-scatter.4
  301.3 137.0 reduce-scatter.2

commit v2 on v1

--- a/solution.py
+++ b/solution.py
@@ -64,11 +64,146 @@
     return AT_TWO + (block - 4 - CHUNKS) * D * SUB + tile, SUB
 
 
-def unpack(gathered, flat, mats, vecs):
-    devices, rows = gathered.shape[0], gathered.shape[1]
-
-    def widen(device, carry):
-        flat[pl.ds(device * rows, rows), :] = gathered[device].astype(F32)
+def part_order(part, bits):
+    order = list(range(bits))
+    if part == 1 and bits > 2:
+        order[1], order[2] = 2, 1
+    return order
+
+
+def owner_of(part, bits, position):
+    owner = 0
+    for place, bit in enumerate(part_order(part, bits)):
+        owner = owner + (position // 2 ** (bits - 1 - place)) % 2 * 2**bit
+    return owner
+
+
+def position_of(part, bits, device):
+    position = 0
+    for place, bit in enumerate(part_order(part, bits)):
+        position = position + device // 2**bit % 2 * 2 ** (bits - 1 - place)
+    return position
+
+
+def meet(bits, me):
+    barrier = pltpu.get_barrier_semaphore()
+    for bit in range(bits):
+        pl.semaphore_signal(
+            barrier, inc=1, device_id=(across(me, bit),), device_id_type=pl.DeviceIdType.MESH
+        )
+    pl.semaphore_wait(barrier, bits)
+
+
+def across(me, bit):
+    return me + 2**bit * (1 - 2 * (me // 2**bit % 2))
+
+
+def gather_kernel(bits, *refs):
+    pairs = LAYERS * 2
+    own, out = refs[:pairs], refs[pairs : 2 * pairs]
+    local_sem, send_sem, recv_sem = refs[2 * pairs :]
+    me = lax.axis_index("fsdp")
+    spots = [position_of(index % 2, bits, me) for index in range(pairs)]
+    locals_ = []
+    for index in range(pairs):
+        copy = pltpu.make_async_copy(own[index], out[index].at[spots[index]], local_sem.at[index])
+        copy.start()
+        locals_.append(copy)
+    meet(bits, me)
+    for copy in locals_:
+        copy.wait()
+    sends = []
+
+    def send(index, step):
+        bit = part_order(index % 2, bits)[bits - 1 - step]
+        size = 2**step
+        region = out[index].at[pl.ds(spots[index] // size * size, size)]
+        copy = pltpu.make_async_remote_copy(
+            src_ref=region,
+            dst_ref=region,
+            send_sem=send_sem.at[index, step],
+            recv_sem=recv_sem.at[index, step],
+            device_id=(across(me, bit),),
+            device_id_type=pl.DeviceIdType.MESH,
+        )
+        copy.start()
+        sends.append(copy)
+        return copy
+
+    flying = [send(index, 0) for index in range(pairs)]
+    for step in range(bits):
+        for index in range(pairs):
+            flying[index].wait_recv()
+            if step + 1 < bits:
+                flying[index] = send(index, step + 1)
+    for copy in sends:
+        copy.wait_send()
+
+
+def scatter_kernel(bits, *refs):
+    pairs = LAYERS * 2
+    packed, out = refs[:pairs], refs[pairs : pairs + LAYERS]
+    landed = refs[pairs + LAYERS : pairs + LAYERS + pairs * bits]
+    send_sem, recv_sem = refs[pairs + LAYERS + pairs * bits :]
+    me = lax.axis_index("fsdp")
+    meet(bits, me)
+    sends = []
+
+    def source(index, step):
+        return packed[index] if step == 0 else landed[index * bits + step - 1]
+
+    def mine(index, step):
+        return me // 2 ** part_order(index % 2, bits)[step] % 2
+
+    def send(index, step):
+        half = 2 ** (bits - 1 - step)
+        copy = pltpu.make_async_remote_copy(
+            src_ref=source(index, step).at[pl.ds((1 - mine(index, step)) * half, half)],
+            dst_ref=landed[index * bits + step],
+            send_sem=send_sem.at[index, step],
+            recv_sem=recv_sem.at[index, step],
+            device_id=(across(me, part_order(index % 2, bits)[step]),),
+            device_id_type=pl.DeviceIdType.MESH,
+        )
+        copy.start()
+        sends.append(copy)
+        return copy
+
+    flying = [send(index, 0) for index in range(pairs)]
+    for step in range(bits):
+        half = 2 ** (bits - 1 - step)
+        for index in range(pairs):
+            flying[index].wait_recv()
+            here, before = landed[index * bits + step], source(index, step)
+            base = mine(index, step) * half
+            if step + 1 < bits:
+
+                def add(block, carry, here=here, before=before, base=base):
+                    here[block] = (here[block].astype(F32) + before[base + block].astype(F32)).astype(
+                        BF16
+                    )
+                    return carry
+
+                lax.fori_loop(0, half, add, 0)
+                flying[index] = send(index, step + 1)
+            else:
+                rows = here.shape[1]
+                start = 0 if index % 2 == 0 else out[0].shape[0] - rows
+                out[index // 2][start : start + rows, :] = here[0].astype(F32) + before[base].astype(F32)
+    for copy in sends:
+        copy.wait_send()
+
+
+def unpack(gathered, owned, flat, mats, vecs):
+    devices = gathered[0].shape[0]
+    bits = devices.bit_length() - 1
+    top = gathered[0].shape[1]
+
+    def widen(position, carry):
+        first = owner_of(0, bits, position) * owned
+        flat[pl.ds(first, top), :] = gathered[0][position].astype(F32)
+        second = owner_of(1, bits, position) * owned + top
+        flat[pl.ds(second, owned - top), :] = gathered[1][position].astype(F32)[: owned - top]
         return carry
 
     lax.fori_loop(0, devices, widen, 0)
@@ -238,14 +373,19 @@
 
 
 def send_out(flat, packed):
-    devices, rows = packed.shape[0], packed.shape[1]
+    devices, top = packed[0].shape[0], packed[0].shape[1]
+    bits = devices.bit_length() - 1
     owned = flat.shape[0] // devices
+    spare = top + packed[1].shape[1] - owned
     flat[USED:, :] = jnp.zeros((flat.shape[0] - USED, LANES), F32)
 
-    def narrow(device, carry):
-        packed[device, :owned, :] = flat[pl.ds(device * owned, owned), :].astype(BF16)
-        if rows > owned:
-            packed[device, owned:, :] = jnp.zeros((rows - owned, LANES), BF16)
+    def narrow(position, carry):
+        first = owner_of(0, bits, position) * owned
+        packed[0][position] = flat[pl.ds(first, top), :].astype(BF16)
+        second = owner_of(1, bits, position) * owned + top
+        packed[1][position, : owned - top, :] = flat[pl.ds(second, owned - top), :].astype(BF16)
+        if spare > 0:
+            packed[1][position, owned - top :, :] = jnp.zeros((spare, LANES), BF16)
         return carry
 
     lax.fori_loop(0, devices, narrow, 0)
@@ -268,16 +408,16 @@
 WEIGHTS = [((BLOCKS, D, D), BF16), ((16, D), F32)]
 
 
-def first_kernel(slots, gathered, stream, *rest):
+def first_kernel(slots, owned, top, bottom, stream, *rest):
     mats, vecs, *saves = rest[:10]
     result, flat = rest[10:]
-    unpack(gathered, flat, mats, vecs)
+    unpack((top, bottom), owned, flat, mats, vecs)
     result[...] = forward(slots, stream, mats, vecs, saves)
 
 
-def turn_kernel(slots, gathered, stream, upstream, result, down, packed, *rest):
-    flat, mixed, att_grad, mats, vecs, *saves = rest
-    unpack(gathered, flat, mats, vecs)
+def turn_kernel(slots, owned, top, bottom, stream, upstream, result, down, *rest):
+    packed, (flat, mixed, att_grad, mats, vecs, *saves) = rest[:2], rest[2:]
+    unpack((top, bottom), owned, flat, mats, vecs)
     result[...] = forward(slots, stream, mats, vecs, saves)
     down[...] = backward(
         slots, upstream, stream, mats, vecs, saves, flat, mixed, att_grad
@@ -287,13 +427,13 @@
 
 def last_kernel(slots, upstream, stream, *rest):
     mats, vecs, *saved = rest[:10]
-    down, packed, flat, mixed, att_grad, middle = rest[10:]
+    down, top, bottom, flat, mixed, att_grad, middle = rest[10:]
     middle[...] = saved[5][...]
     saved[5] = middle
     down[...] = backward(
         slots, upstream, stream, mats, vecs, saved, flat, mixed, att_grad
     )
-    send_out(flat, packed)
+    send_out(flat, (top, bottom))
 
 
 def shapes(listed):
@@ -304,16 +444,17 @@
     return [pltpu.VMEM(extent, kind) for extent, kind in listed]
 
 
-def call(body, args, outs, scratches, flops):
+def call(body, args, outs, scratches, flops, ident=None):
     whole = pl.BlockSpec(memory_space=pltpu.VMEM)
+    extra = {} if ident is None else dict(collective_id=ident, has_side_effects=True)
     return pl.pallas_call(
         body,
         out_shape=shapes(outs),
         in_specs=[whole] * len(args),
         out_specs=[whole] * len(outs),
-        scratch_shapes=scratch(scratches),
+        scratch_shapes=scratches,
         cost_estimate=pl.CostEstimate(flops=flops, bytes_accessed=12000000, transcendentals=0),
-        compiler_params=pltpu.CompilerParams(vmem_limit_bytes=60000000),
+        compiler_params=pltpu.CompilerParams(vmem_limit_bytes=60000000, **extra),
     )(*args)
 
 
@@ -328,64 +469,80 @@
     return (updated, first_new, second_new)
 
 
-def as_tiles(shard_vec):
-    return shard_vec.astype(jnp.bfloat16).reshape(-1, LANES)
-
-
 def on_device(images, cotangent, counts, params, moment_one, moment_two):
     slots = images.shape[0]
     shard_len = params.shape[1]
     devices = lax.axis_size("fsdp")
     owned = shard_len // LANES
+    bits = devices.bit_length() - 1
     padded = -(-owned // 16) * 16
+    top = padded // 32 * 16
     tokens = slots * ROWS
     flat_rows = owned * devices
     live = (jnp.arange(slots) < counts[0]).astype(F32)[:, None, None]
-    gathered = [
-        lax.all_gather(as_tiles(params[position]), "fsdp", axis=0) for position in range(LAYERS)
-    ]
+    own = jnp.pad(
+        params.astype(BF16).reshape(LAYERS, owned, LANES), ((0, 0), (0, padded - owned), (0, 0))
+    )
+    halves = [((devices, top, LANES), BF16), ((devices, padded - top, LANES), BF16)]
+    many = (LAYERS * 2, bits)
+    gathered = call(
+        functools.partial(gather_kernel, bits),
+        [piece for position in range(LAYERS) for piece in (own[position, :top], own[position, top:])],
+        halves * LAYERS,
+        [
+            pltpu.SemaphoreType.DMA((LAYERS * 2,)),
+            pltpu.SemaphoreType.DMA(many),
+            pltpu.SemaphoreType.DMA(many),
+        ],
+        0,
+        0,
+    )
     widen = ((0, 0), (0, ROWS - SEQ), (0, 0))
     start = jnp.pad(images, widen).reshape(tokens, D)
     upstream = jnp.pad(cotangent * live, widen).reshape(tokens, D)
 
     saves = save_shapes(slots)
     rows_out = ((tokens, D), F32)
-    packed_out = ((devices, padded, LANES), BF16)
     flat = ((flat_rows, LANES), F32)
     back = [flat, ((3, tokens, D), BF16), ((tokens, D), BF16)]
     flops = 2 * tokens * USED * LANES
 
     *kept, stream = call(
-        functools.partial(first_kernel, slots),
-        [gathered[0], start],
+        functools.partial(first_kernel, slots, owned),
+        [*gathered[:2], start],
         WEIGHTS + saves + [rows_out],
-        [flat],
+        scratch([flat]),
         flops,
     )
-    result, down, packed_one = call(
-        functools.partial(turn_kernel, slots),
-        [gathered[1], stream, upstream],
-        [rows_out, rows_out, packed_out],
-        back + WEIGHTS + saves,
+    result, down, *packed_one = call(
+        functools.partial(turn_kernel, slots, owned),
+        [*gathered[2:], stream, upstream],
+        [rows_out, rows_out] + halves,
+        scratch(back + WEIGHTS + saves),
         3 * flops,
     )
-    down, packed_zero = call(
+    down, *packed_zero = call(
         functools.partial(last_kernel, slots),
         [down, start] + kept,
-        [rows_out, packed_out],
-        back + [rows_out],
+        [rows_out] + halves,
+        scratch(back + [rows_out]),
         2 * flops,
     )
-    grad_stack = jnp.stack(
-        [
-            lax.psum_scatter(
-                packed.reshape(devices * padded, LANES), "fsdp", scatter_dimension=0, tiled=True
-            )[:owned]
-            .astype(F32)
-            .reshape(-1)
-            for packed in (packed_zero, packed_one)
-        ]
-    )
+    landing = [
+        ((2 ** (bits - 1 - step), rows, LANES), BF16)
+        for _ in range(LAYERS)
+        for rows in (top, padded - top)
+        for step in range(bits)
+    ]
+    sums = call(
+        functools.partial(scatter_kernel, bits),
+        [*packed_zero, *packed_one],
+        [((padded, LANES), F32)] * LAYERS,
+        scratch(landing) + [pltpu.SemaphoreType.DMA(many), pltpu.SemaphoreType.DMA(many)],
+        0,
+        1,
+    )
+    grad_stack = jnp.stack([total[:owned].reshape(-1) for total in sums])
     updated, first_new, second_new = adamw(params, moment_one, moment_two, grad_stack)
     return (
         result.reshape(slots, ROWS, D)[:, :SEQ] * live,

time: 449 us -> 181 us (0.40)
  waiting for transfers between devices: 367 us -> 0 us
  Pallas kernels: 51.1 us -> 169 us
  between operations: 14.5 us -> 1.53 us
  local copies, waits for them, and re-layouts: 9.06 us -> 4.55 us
    reduce_scatter x2 -> x0, waiting for transfers between devices: 258 us -> none  [on_device(): lax.psum_scatter(packed.reshape(devices * padded, LANES), 'fsdp', scatter...]
    pallas_call x3 -> x5, Pallas kernels: 51.1 us -> 169 us  [call(): pl.pallas_call(body, out_shape=shapes(outs), in_specs=[whole] * len(args)...]
    all_gather x2 -> x0, waiting for transfers between devices: 109 us -> none  [on_device(): lax.all_gather(as_tiles(params[position]), 'fsdp', axis=0)]
  transfers between devices with their start and end apart: 4 -> 0, of which waited for: 4 -> 0; matrix products, arithmetic and copies ran while one was open for 2% -> 0% of each run, Pallas kernels for 6% -> 0%
where the time goes in v2:
time: 181 us; the launch traced here: 180 us
  Pallas kernels  169 us (93%)
  other arithmetic  5.62 us (3%)
  local copies, waits for them, and re-layouts  4.55 us (3%)
    pallas_call x5, Pallas kernels, call(): pl.pallas_call(body, out_shape=shapes(outs), in_specs=[whole] * len(args)...  169 us

profile of v2, /device:TPU:0, one launch (start us, length us, event | category | flops | bytes accessed | tf_op | source)
XLA Modules:
  0.0 180.5 jit_solution(3837816716411358216)
XLA Ops:
  0.6 0.0 copy-start.1
  0.6 0.0 copy-start.6
  1.4 1.2 convert_element_type.16
  2.6 0.4 reshape.32
  2.9 0.7 fusion.2
  3.6 0.0 copy-done.6
  3.7 0.8 pad.13.clone
  4.4 0.0 copy-done.1
  4.4 0.3 broadcast_multiply_fusion
  4.8 0.9 pad.14.clone
  5.7 57.4 %shard_map.109 = (bf16[32,224,128]{2,1,0:T(8,128)(2,1)}, bf16[32,224,128]{2,1,0:T(8,128)(2,1)}, bf16[32,224,128]{2,1,0:T(8,128)(2,1)}, bf16[32,224,128]{2,1,0:T(8,128)(2,1)}) custom-call(bf16[224,128]{1,0:T(8,128)(2,1)} %get-tuple-element.61.refs_0_, bf16[224,128]{1,0:T(8,128)(2,1)} %get-tuple-element.60.refs_1_, ...), custom_call_target="tpu_custom_call" | custom-call | bytes 12000000 | tf_op jit(solution)/shard_map/pallas_call | solution.py:450
  63.1 13.2 %shard_map.110 = (bf16[12,384,384]{2,1,0:T(8,128)(2,1)}, f32[16,384]{1,0:T(8,128)}, bf16[416,384]{1,0:T(8,128)(2,1)}, bf16[416,384]{1,0:T(8,128)(2,1)}, bf16[416...) custom-call(bf16[32,224,128]{2,1,0:T(8,128)(2,1)} %get-tuple-element, ...), custom_call_target="tpu_custom_call" | custom-call | flops 1476034560 | bytes 12000000 | tf_op jit(solution)/shard_map/pallas_call | solution.py:450
  76.3 24.3 %shard_map.111 = (f32[416,384]{1,0:T(8,128)}, f32[416,384]{1,0:T(8,128)}, bf16[32,224,128]{2,1,0:T(8,128)(2,1)}, bf16[32,224,128]{2,1,0:T(8,128)(2,1)}) custom-call(bf16[32,224,128]{2,1,0:T(8,128)(2,1)} %get-tuple-element.30.top, bf16[32,224,128]{2,1,0:T(8,128)(2,1)} %get-tuple-element.31.bottom, f32[416,384]{1,0:T(8,128)} %get-tuple-element.34.stream, ...), custom_call_target="tpu_custom_call" | custom-call | flops 4428103680 | bytes 12000000 | tf_op jit(solution)/shard_map/pallas_call | solution.py:450
  100.6 0.0 copy-start.3
  100.6 17.2 %shard_map.112 = (f32[416,384]{1,0:T(8,128)}, bf16[32,224,128]{2,1,0:T(8,128)(2,1)}, bf16[32,224,128]{2,1,0:T(8,128)(2,1)}) custom-call(f32[416,384]{1,0:T(8,128)} %get-tuple-element.36.upstream, bf16[416,384]{1,0:T(8,128)(2,1)} %bitcast.27, bf16[12,384,384]{2,1,0:T(8,128)(2,1)} %get-tuple-element.37.rest_0_, f32[16,384]{1,0:T(8,128)} %get-tuple-element.38.rest_1_, ...), custom_call_target="tpu_custom_call" | custom-call | flops 2952069120 | bytes 12000000 | tf_op jit(solution)/shard_map/pallas_call | solution.py:450
  117.8 0.0 copy-done.3
  117.8 1.2 copy_multiply_fusion
  119.0 0.0 copy-start.2
  119.0 56.7 %shard_map.113 = (f32[448,128]{1,0:T(8,128)}, f32[448,128]{1,0:T(8,128)}) custom-call(bf16[32,224,128]{2,1,0:T(8,128)(2,1)} %get-tuple-element.48.refs_0_, bf16[32,224,128]{2,1,0:T(8,128)(2,1)} %get-tuple-element.49.refs_1_, bf16[32,224,128]{2,1,0:T(8,128)(2,1)} %get-tuple-element.50.refs_2_, bf16[32,224,128]{2,1,0:T(8,128)(2,1)} %get-tuple-element.51.refs_3_), custom_call_target="tpu_custom_call" | custom-call | bytes 12000000 | tf_op jit(solution)/shard_map/pallas_call | solution.py:450
  175.7 0.0 copy-start.7
  175.7 0.0 copy-start.8
  175.7 0.0 copy-done.2
  175.7 0.0 copy-start
  175.7 0.0 copy-start.4
  175.7 0.0 copy-start.5
  175.8 1.1 copy.21
  176.9 0.0 copy-done.7
  176.9 0.0 copy-done.8
  177.0 0.2 copy.29
  177.2 0.2 copy.30
  177.5 0.0 copy-done
  177.5 0.0 copy-done.4
  177.5 0.0 copy-done.5
  177.5 3.0 %multiply_subtract_fusion = (f32[2,55552]{1,0:T(2,128)}, f32[2,55552]{1,0:T(2,128)}, f32[2,55552]{1,0:T(2,128)}, f32[2,55552]{1,0:T(2,128)}) fusion(f32[2,55552]{1,0:T(2,128)S(1)} %copy-done, f32[2,55552]{1,0:T(2,128)S(1)} %copy-done.4, f32[2,55552]{1,0:T(2,128)S(1)} %copy-done.5, f32[1,55552]{1,0:T(1,128)S(1)} %bitcast.28, f32[1,55552]{1,0:T(1,128)S(1)} %bitcast.29), kind=kLoop, calls=%fused_computation.4 | loop fusion | flops 1777664 | bytes 3555328 | tf_op jit(solution)/shard_map/sub | solution.py:466
  (6 shorter events, 0.2 us)
Async XLA Ops:
  0.6 3.8 %copy-start.1 = (f32[2,197,384]{2,0,1:T(2,128)S(1)}, f32[2,197,384]{2,0,1:T(2,128)}, u32[]{:S(2)}) copy-start(f32[2,197,384]{2,0,1:T(2,128)} %param.7) | copy-start | bytes 1815556
  0.6 3.0 %copy-start.6 = (bf16[2,197,384]{2,0,1:T(2,128)(2,1)S(1)}, bf16[2,197,384]{2,0,1:T(2,128)(2,1)}, u32[]{:S(2)}) copy-start(bf16[2,197,384]{2,0,1:T(2,128)(2,1)} %param.6) | copy-start | bytes 907780
  100.6 17.2 %copy-start.3 = (f32[416,384]{1,0:T(8,128)S(1)}, f32[416,384]{1,0:T(8,128)}, u32[]{:S(2)}) copy-start(f32[416,384]{1,0:T(8,128)} %get-tuple-element.35) | copy-start | bytes 1916932
  119.0 56.7 %copy-start.2 = (f32[416,384]{1,0:T(8,128)S(1)}, f32[416,384]{1,0:T(8,128)}, u32[]{:S(2)}) copy-start(f32[416,384]{1,0:T(8,128)} %get-tuple-element.47) | copy-start | bytes 1916932
  175.7 1.3 copy-start.7
  175.7 1.2 copy-start.8
  175.7 1.7 copy-start
  175.7 1.7 copy-start.4
  175.7 1.7 copy-start.5

commit v3 on v2

--- a/solution.py
+++ b/solution.py
@@ -98,10 +98,8 @@
     return me + 2**bit * (1 - 2 * (me // 2**bit % 2))
 
 
-def gather_kernel(bits, *refs):
+def gather_steps(bits, own, out, local_sem, send_sem, recv_sem):
     pairs = LAYERS * 2
-    own, out = refs[:pairs], refs[pairs : 2 * pairs]
-    local_sem, send_sem, recv_sem = refs[2 * pairs :]
     me = lax.axis_index("fsdp")
     spots = [position_of(index % 2, bits, me) for index in range(pairs)]
     locals_ = []
@@ -131,13 +129,23 @@
         return copy
 
     flying = [send(index, 0) for index in range(pairs)]
-    for step in range(bits):
-        for index in range(pairs):
+    schedule = [(index, step) for step in range(bits - 2) for index in range(pairs)]
+    schedule += [(index, step) for step in (bits - 2, bits - 1) for index in range(2)]
+    for index, step in schedule:
+        flying[index].wait_recv()
+        if step + 1 < bits:
+            flying[index] = send(index, step + 1)
+    yield
+    for step in (bits - 2, bits - 1):
+        for index in range(2, pairs):
             flying[index].wait_recv()
             if step + 1 < bits:
                 flying[index] = send(index, step + 1)
+        if step == bits - 2:
+            yield
     for copy in sends:
         copy.wait_send()
+    yield
 
 
 def scatter_kernel(bits, *refs):
@@ -260,7 +268,7 @@
     return jnp.where(lane_pick(half), value, jnp.zeros_like(value))
 
 
-def forward(slots, stream, mats, vecs, saves):
+def forward(slots, stream, mats, vecs, saves, tick=None):
     query, key, value, attended, exact, middle, slope, hidden = saves
 
     def vec(index):
@@ -290,6 +298,8 @@
         return carry
 
     lax.fori_loop(0, HEADS // 2, heads, 0)
+    if tick is not None:
+        tick()
     middle[...] = stream[...].astype(F32) + nn(attended[...], mats[3]) + vec(B_OUT)
     normed, _ = normalize(middle[...])
     act = (normed * vec(G_TWO) + vec(B_TWO)).astype(BF16)
@@ -408,11 +418,16 @@
 WEIGHTS = [((BLOCKS, D, D), BF16), ((16, D), F32)]
 
 
-def first_kernel(slots, owned, top, bottom, stream, *rest):
-    mats, vecs, *saves = rest[:10]
-    result, flat = rest[10:]
-    unpack((top, bottom), owned, flat, mats, vecs)
-    result[...] = forward(slots, stream, mats, vecs, saves)
+def first_kernel(slots, owned, bits, *refs):
+    own, stream, after = refs[:4], refs[4], refs[5:7]
+    mats, vecs, *saves = refs[7:17]
+    result, flat = refs[17:19]
+    before = refs[19:21]
+    steps = gather_steps(bits, own, [*before, *after], *refs[21:])
+    next(steps)
+    unpack(before, owned, flat, mats, vecs)
+    result[...] = forward(slots, stream, mats, vecs, saves, lambda: next(steps))
+    next(steps)
 
 
 def turn_kernel(slots, owned, top, bottom, stream, upstream, result, down, *rest):
@@ -485,18 +500,6 @@
     )
     halves = [((devices, top, LANES), BF16), ((devices, padded - top, LANES), BF16)]
     many = (LAYERS * 2, bits)
-    gathered = call(
-        functools.partial(gather_kernel, bits),
-        [piece for position in range(LAYERS) for piece in (own[position, :top], own[position, top:])],
-        halves * LAYERS,
-        [
-            pltpu.SemaphoreType.DMA((LAYERS * 2,)),
-            pltpu.SemaphoreType.DMA(many),
-            pltpu.SemaphoreType.DMA(many),
-        ],
-        0,
-        0,
-    )
     widen = ((0, 0), (0, ROWS - SEQ), (0, 0))
     start = jnp.pad(images, widen).reshape(tokens, D)
     upstream = jnp.pad(cotangent * live, widen).reshape(tokens, D)
@@ -507,16 +510,23 @@
     back = [flat, ((3, tokens, D), BF16), ((tokens, D), BF16)]
     flops = 2 * tokens * USED * LANES
 
-    *kept, stream = call(
-        functools.partial(first_kernel, slots, owned),
-        [*gathered[:2], start],
-        WEIGHTS + saves + [rows_out],
-        scratch([flat]),
+    after_top, after_bottom, *kept, stream = call(
+        functools.partial(first_kernel, slots, owned, bits),
+        [piece for position in range(LAYERS) for piece in (own[position, :top], own[position, top:])]
+        + [start],
+        halves + WEIGHTS + saves + [rows_out],
+        scratch([flat] + halves)
+        + [
+            pltpu.SemaphoreType.DMA((LAYERS * 2,)),
+            pltpu.SemaphoreType.DMA(many),
+            pltpu.SemaphoreType.DMA(many),
+        ],
         flops,
+        0,
     )
     result, down, *packed_one = call(
         functools.partial(turn_kernel, slots, owned),
-        [*gathered[2:], stream, upstream],
+        [after_top, after_bottom, stream, upstream],
         [rows_out, rows_out] + halves,
         scratch(back + WEIGHTS + saves),
         3 * flops,

time: 181 us -> 172 us (0.950)
  Pallas kernels: 169 us -> 161 us
    pallas_call x5 -> x4, Pallas kernels: 169 us -> 161 us  [call(): pl.pallas_call(body, out_shape=shapes(outs), in_specs=[whole] * len(args)...]
where the time goes in v3:
time: 172 us
  Pallas kernels  161 us (94%)
  other arithmetic  5.62 us (3%)
  local copies, waits for them, and re-layouts  4.52 us (3%)
    pallas_call x4, Pallas kernels, call(): pl.pallas_call(body, out_shape=shapes(outs), in_specs=[whole] * len(args)...  161 us

profile of v3, /device:TPU:0, one launch (start us, length us, event | category | flops | bytes accessed | tf_op | source)
XLA Modules:
  0.0 172.2 jit_solution(5981338055668578214)
XLA Ops:
  0.6 0.0 copy-start.1
  0.6 0.0 copy-start.6
  1.4 1.2 convert_element_type.16
  2.6 0.4 reshape.32
  2.9 0.7 fusion.2
  3.6 0.0 copy-done.6
  3.7 0.8 pad.13.clone
  4.4 0.0 copy-done.1
  4.4 0.3 broadcast_multiply_fusion
  4.8 0.9 pad.14.clone
  5.6 63.4 %shard_map.109 = (bf16[32,224,128]{2,1,0:T(8,128)(2,1)}, bf16[32,224,128]{2,1,0:T(8,128)(2,1)}, bf16[12,384,384]{2,1,0:T(8,128)(2,1)}, f32[16,384]{1,0:T(8,128)}...) custom-call(bf16[224,128]{1,0:T(8,128)(2,1)} %get-tuple-element.57.r, ...), custom_call_target="tpu_custom_call" | custom-call | flops 1476034560 | bytes 12000000 | tf_op jit(solution)/shard_map/pallas_call | solution.py:465
  69.0 24.2 %shard_map.110 = (f32[416,384]{1,0:T(8,128)}, f32[416,384]{1,0:T(8,128)}, bf16[32,224,128]{2,1,0:T(8,128)(2,1)}, bf16[32,224,128]{2,1,0:T(8,128)(2,1)}) custom-call(bf16[32,224,128]{2,1,0:T(8,128)(2,1)} %get-tuple-element.28.top, bf16[32,224,128]{2,1,0:T(8,128)(2,1)} %get-tuple-element.29.bottom, f32[416,384]{1,0:T(8,128)} %get-tuple-element.30.stream, ...), custom_call_target="tpu_custom_call" | custom-call | flops 4428103680 | bytes 12000000 | tf_op jit(solution)/shard_map/pallas_call | solution.py:465
  93.2 0.0 copy-start.3
  93.3 17.2 %shard_map.111 = (f32[416,384]{1,0:T(8,128)}, bf16[32,224,128]{2,1,0:T(8,128)(2,1)}, bf16[32,224,128]{2,1,0:T(8,128)(2,1)}) custom-call(f32[416,384]{1,0:T(8,128)} %get-tuple-element.32.upstream, bf16[416,384]{1,0:T(8,128)(2,1)} %bitcast.27, bf16[12,384,384]{2,1,0:T(8,128)(2,1)} %get-tuple-element.33.rest_0_, f32[16,384]{1,0:T(8,128)} %get-tuple-element.34.rest_1_, ...), custom_call_target="tpu_custom_call" | custom-call | flops 2952069120 | bytes 12000000 | tf_op jit(solution)/shard_map/pallas_call | solution.py:465
  110.5 0.0 copy-done.3
  110.5 1.2 copy_multiply_fusion
  111.7 0.0 copy-start.2
  111.7 55.7 %shard_map.112 = (f32[448,128]{1,0:T(8,128)}, f32[448,128]{1,0:T(8,128)}) custom-call(bf16[32,224,128]{2,1,0:T(8,128)(2,1)} %get-tuple-element.44.refs_0_, bf16[32,224,128]{2,1,0:T(8,128)(2,1)} %get-tuple-element.45.refs_1_, bf16[32,224,128]{2,1,0:T(8,128)(2,1)} %get-tuple-element.46.refs_2_, bf16[32,224,128]{2,1,0:T(8,128)(2,1)} %get-tuple-element.47.refs_3_), custom_call_target="tpu_custom_call" | custom-call | bytes 12000000 | tf_op jit(solution)/shard_map/pallas_call | solution.py:465
  167.5 0.0 copy-start.7
  167.5 0.0 copy-start.8
  167.5 0.0 copy-done.2
  167.5 0.0 copy-start
  167.5 0.0 copy-start.4
  167.5 0.0 copy-start.5
  167.6 1.1 copy.21
  168.7 0.0 copy-done.7
  168.7 0.0 copy-done.8
  168.8 0.2 copy.29
  169.0 0.2 copy.30
  169.2 0.0 copy-done
  169.2 0.0 copy-done.4
  169.2 0.0 copy-done.5
  169.3 3.0 %multiply_subtract_fusion = (f32[2,55552]{1,0:T(2,128)}, f32[2,55552]{1,0:T(2,128)}, f32[2,55552]{1,0:T(2,128)}, f32[2,55552]{1,0:T(2,128)}) fusion(f32[2,55552]{1,0:T(2,128)S(1)} %copy-done, f32[2,55552]{1,0:T(2,128)S(1)} %copy-done.4, f32[2,55552]{1,0:T(2,128)S(1)} %copy-done.5, f32[1,55552]{1,0:T(1,128)S(1)} %bitcast.28, f32[1,55552]{1,0:T(1,128)S(1)} %bitcast.29), kind=kLoop, calls=%fused_computation.4 | loop fusion | flops 1777664 | bytes 3555328 | tf_op jit(solution)/shard_map/sub | solution.py:481
  (6 shorter events, 0.2 us)
Async XLA Ops:
  0.6 3.8 %copy-start.1 = (f32[2,197,384]{2,0,1:T(2,128)S(1)}, f32[2,197,384]{2,0,1:T(2,128)}, u32[]{:S(2)}) copy-start(f32[2,197,384]{2,0,1:T(2,128)} %param.7) | copy-start | bytes 1815556
  0.6 3.0 %copy-start.6 = (bf16[2,197,384]{2,0,1:T(2,128)(2,1)S(1)}, bf16[2,197,384]{2,0,1:T(2,128)(2,1)}, u32[]{:S(2)}) copy-start(bf16[2,197,384]{2,0,1:T(2,128)(2,1)} %param.6) | copy-start | bytes 907780
  93.2 17.2 %copy-start.3 = (f32[416,384]{1,0:T(8,128)S(1)}, f32[416,384]{1,0:T(8,128)}, u32[]{:S(2)}) copy-start(f32[416,384]{1,0:T(8,128)} %get-tuple-element.31) | copy-start | bytes 1916932
  111.7 55.8 %copy-start.2 = (f32[416,384]{1,0:T(8,128)S(1)}, f32[416,384]{1,0:T(8,128)}, u32[]{:S(2)}) copy-start(f32[416,384]{1,0:T(8,128)} %get-tuple-element.43) | copy-start | bytes 1916932
  167.5 1.3 copy-start.7
  167.5 1.2 copy-start.8
  167.5 1.7 %copy-start = (f32[2,55552]{1,0:T(2,128)S(1)}, f32[2,55552]{1,0:T(2,128)}, u32[]{:S(2)}) copy-start(f32[2,55552]{1,0:T(2,128)} %param.9) | copy-start | bytes 1333252
  167.5 1.7 %copy-start.4 = (f32[2,55552]{1,0:T(2,128)S(1)}, f32[2,55552]{1,0:T(2,128)}, u32[]{:S(2)}) copy-start(f32[2,55552]{1,0:T(2,128)} %param.10) | copy-start | bytes 1333252
  167.5 1.7 %copy-start.5 = (f32[2,55552]{1,0:T(2,128)S(1)}, f32[2,55552]{1,0:T(2,128)}, u32[]{:S(2)}) copy-start(f32[2,55552]{1,0:T(2,128)} %param.11) | copy-start | bytes 1333252
